TPU v7x, 128 devices: a whole 4x4x4 slice. The times are simulated.
128 devices in a mesh: grp: 8 (over x, z_hi), fac: 16 (over y, z_lo, core).
Axes of the slice: x: 4, y: 4, z: 4 (z_hi: 2, z_lo: 2; z = z_hi * 2 + z_lo), core: 2. Of those that a mesh axis runs over, the one named last changes fastest.
Arguments:
- metric_panels: bfloat16 [32768, 2048], P('fac'), may hold values from -0.1875 to 0.1875
- diag_inverses: float32 [2, 1024, 1024], replicated, as said below
- pair_batch: bfloat16 [32768, 8192], P('fac', 'grp'), may hold values from -6 to 6
Outputs:
- solved: bfloat16 [32768, 8192], P('fac', 'grp')
Inputs may be any that keep to these rules, and one draw needn't show every extreme that they name: `diag_inverses`: each of the two blocks is lower triangular with a positive diagonal.
All inputs are finite; a program needn't handle non-finite values.
Results may differ from a plain program's by a relative error of at most 0.006.
Values may be sent and summed in bfloat16 or wider, within the bound.
No kernel may reach another device: no remote copies, remote signals or barrier semaphores. Data moves between devices by JAX's collectives and lax.ppermute only.
A program may use at most 128 MiB of HBM per device.

v0:
```python
import jax
import jax.numpy as jnp
from jax import lax
from jax.sharding import PartitionSpec as P


def spread(value, axis, source):
    kept = jnp.where(lax.axis_index(axis) == source, value, 0).astype(value.dtype)
    return lax.psum(kept, axis)


def times_transposed(left, right):
    return lax.dot_general(
        left,
        right,
        (((1,), (1,)), ((), ())),
        precision=lax.Precision.HIGHEST,
        preferred_element_type=jnp.float32,
    )


def product(left, right):
    return jnp.dot(left, right, precision=lax.Precision.HIGHEST, preferred_element_type=jnp.float32)


def gather_factor(piece):
    return lax.all_gather(piece, "grp", axis=0, tiled=True)


def body(metric_panels, diag_inverses, pair_batch):
    panel_size = diag_inverses.shape[1]
    pair_count = pair_batch.shape[1]
    local_rows = pair_batch.shape[0]
    first_inverse = diag_inverses[0]
    second_inverse = diag_inverses[1]
    fac_index = lax.axis_index("fac")
    empty = jnp.zeros((panel_size, pair_count), jnp.float32)
    share_rows = local_rows // lax.axis_size("grp")
    row_start = lax.axis_index("grp") * share_rows
    own_metric = lax.dynamic_slice_in_dim(metric_panels, row_start, share_rows, 0).astype(
        jnp.float32
    )
    first_share = times_transposed(own_metric[:, :panel_size], first_inverse)
    factor_first = gather_factor(first_share)
    cross_rows = spread(factor_first[panel_size : 2 * panel_size], "fac", 0)
    updated = own_metric[:, panel_size:] - times_transposed(first_share, cross_rows)
    factor_second = gather_factor(times_transposed(updated, second_inverse))

    def solve_first(upper):
        return product(first_inverse, upper.astype(jnp.float32))

    def solve_second(lower, first_solved):
        return product(
            second_inverse, lower.astype(jnp.float32) - product(cross_rows, first_solved)
        )

    def chained_rest(first_solved, second_solved):
        partial_rest = pair_batch.astype(jnp.float32) - product(factor_first, first_solved)
        return partial_rest - product(factor_second, second_solved)

    first_local = lax.cond(
        fac_index == 0, lambda: solve_first(pair_batch[:panel_size]), lambda: empty
    )
    first_solved = spread(first_local, "fac", 0)
    second_local = lax.cond(
        fac_index == 0,
        lambda: solve_second(pair_batch[panel_size : 2 * panel_size], first_solved),
        lambda: empty,
    )
    second_solved = spread(second_local.astype(jnp.bfloat16), "fac", 0).astype(second_local.dtype)
    result = lax.cond(
        fac_index == 0,
        lambda: jnp.concatenate([first_solved, second_solved], axis=0),
        lambda: chained_rest(first_solved, second_solved),
    )
    return result.astype(jnp.bfloat16)


def solution(mesh):
    in_specs = (P("fac", None), P(), P("fac", "grp"))
    out_specs = P("fac", "grp")
    return jax.shard_map(body, mesh=mesh, in_specs=in_specs, out_specs=out_specs, check_vma=False)
```

profile of v0, /device:TPU:1, one launch (start us, length us, event | category | flops | bytes accessed | tf_op | source)
XLA Modules:
  0.0 670.5 jit_solution(1340951626374905802)
XLA Ops:
  6.5 0.0 all-gather.3.cloned.1.call-start
  6.5 5.5 fusion.8
  12.0 0.0 all-gather.3.cloned.1.call-update
  12.1 0.0 all-reduce.6.cloned.1.call-start
  12.1 8.5 %slice_bitcast_fusion = (f32[1024,1024]{1,0:T(8,128)}, f32[1024,1024]{1,0:T(8,128)}) fusion(f32[2,1024,1024]{2,1,0:T(8,128)} %param.10), kind=kLoop, calls=%fused_computation.10 | loop fusion | bytes 16777216 | tf_op jit(solution)/shard_map/squeeze | solution.py:35
  20.6 2.5 conditional.8
  20.6 2.5 broadcast_in_dim.11
  23.1 2.8 broadcast_select_fusion
  25.8 97.3 %all-gather.3.cloned.1.call-done = f32[2048,1024]{1,0:T(8,128)} async-done(((f32[256,1024]{1,0:T(8,128)}), f32[2048,1024]{1,0:T(8,128)}) %all-gather.3.cloned.1.call-update) | async-done | bytes 8388624 | tf_op jit(solution)/shard_map/all_gather | solution.py:27
  123.1 5.0 slice_select_fusion
  128.1 0.0 all-reduce.6.cloned.1.call-update
  128.2 0.0 all-reduce.4.cloned.1.call-start
  128.2 194.1 %all-reduce.6.cloned.1.call-done = (f32[1024,1024]{1,0:T(8,128)}, f32[1024,1024]{1,0:T(8,128)}) async-done(((f32[1024,1024]{1,0:T(8,128)}, f32[1024,1024]{1,0:T(8,128)}), (f32[1024,1024]{1,0:T(8,128)}, f32[1024,1024]{1,0:T(8,128)})) %all-reduce.6.cloned.1.call-update) | async-done | bytes 8388624 | tf_op jit(solution)/shard_map/psum | solution.py:9
  322.3 6.5 conditional.9
  322.3 0.3 broadcast_in_dim.12.clone
  328.8 0.0 copy-start.1
  328.8 1.5 broadcast_select_fusion.1
  330.3 0.0 all-reduce.4.cloned.1.call-update
  330.3 0.0 all-gather.5.cloned.1.call-start
  330.3 0.1 copy-done.1
  330.4 6.0 convolution_subtract_fusion
  336.4 6.9 %fusion.11 = f32[256,1024]{1,0:T(8,128)} fusion(f32[256,1024]{1,0:T(8,128)S(1)} %convolution_subtract_fusion, f32[2,1024,1024]{2,1,0:T(8,128)} %param.10), kind=kOutput, calls=%fused_computation.18 | convolution fusion | flops 3221225472 | bytes 6291456 | tf_op jit(solution)/shard_map/dot_general | solution.py:13
  343.3 0.0 all-gather.5.cloned.1.call-update
  343.3 148.5 %all-reduce.4.cloned.1.call-done = bf16[1024,1024]{1,0:T(8,128)(2,1)} async-done(((bf16[1024,1024]{1,0:T(8,128)(2,1)}), bf16[1024,1024]{1,0:T(8,128)(2,1)}) %all-reduce.4.cloned.1.call-update) | async-done | bytes 2097168 | tf_op jit(solution)/shard_map/psum | solution.py:9
  491.8 4.1 convert_element_type.40
  495.9 107.0 %all-gather.5.cloned.1.call-done = f32[2048,1024]{1,0:T(8,128)} async-done(((f32[256,1024]{1,0:T(8,128)}), f32[2048,1024]{1,0:T(8,128)}) %all-gather.5.cloned.1.call-update) | async-done | bytes 8388624 | tf_op jit(solution)/shard_map/all_gather | solution.py:27
  602.9 60.8 %conditional.10 = (bf16[2048,1024]{1,0:T(8,128)(2,1)}) conditional(s32[]{:T(128)} %convert_element_type.39, (bf16[2048,1024]{1,0:T(8,128)(2,1)}, f32[2048,1024]{1,0:T(8,128)}, f32[1024,1024]{1,0:T(8,128)}, f32[2048,1024]{1,0:T(8,128)}, f32[1024,1024]{1,0:T(8,128)}) %tuple.39, (f32[1024,1024]{1,0:T(8,128)}, f32[1024,1024]{1,0:T(8,128)}) %tuple.40), branch_computations={%region_7.8_spmd, %region_8.9_spmd} | conditional | flops 51547996160 | bytes 117440608
  603.1 0.0 copy-start
  603.1 0.0 copy-start.3
  603.1 0.0 copy-start.5
  603.1 31.1 %fusion.13 = f32[2048,1024]{1,0:T(8,128)S(1)} fusion(f32[2048,1024]{1,0:T(8,128)} %get-tuple-element.54, f32[1024,1024]{1,0:T(8,128)} %get-tuple-element.55), kind=kOutput, calls=%fused_computation.20 | convolution fusion | flops 25769803776 | bytes 20971520 | tf_op jit(solution)/shard_map/cond/branch_0_fun/dot_general | solution.py:23
  634.2 0.0 copy-done
  634.2 0.0 copy-done.3
  634.2 0.0 copy-done.5
  634.2 29.3 %subtract_subtract_fusion = bf16[2048,1024]{1,0:T(8,128)(2,1)} fusion(f32[2048,1024]{1,0:T(8,128)S(1)} %fusion.13, bf16[2048,1024]{1,0:T(8,128)(2,1)S(1)} %copy-done.5, f32[2048,1024]{1,0:T(8,128)S(1)} %copy-done.3, f32[1024,1024]{1,0:T(8,128)S(1)} %copy-done), kind=kOutput, calls=%fused_computation.7 | convolution fusion | flops 25778192384 | bytes 29360128 | tf_op jit(solution)/shard_map/cond/branch_0_fun/dot_general | solution.py:23
Async XLA Ops:
  6.5 116.6 %all-gather.3.cloned.1.call-start = ((), (), s32[]{:S(2)}) async-start(), calls=%async_computation | async-start | bytes 9437184 | tf_op jit(solution)/shard_map/all_gather | solution.py:27
  12.1 310.3 %all-reduce.6.cloned.1.call-start = ((), (), s32[]{:S(2)}) async-start(), calls=%async_computation.3 | async-start | bytes 16777216 | tf_op jit(solution)/shard_map/psum | solution.py:9
  128.2 363.7 %all-reduce.4.cloned.1.call-start = ((), (), s32[]{:S(2)}) async-start(), calls=%async_computation.2 | async-start | bytes 4194304 | tf_op jit(solution)/shard_map/psum | solution.py:9
  328.8 1.6 copy-start.1
  330.3 272.6 %all-gather.5.cloned.1.call-start = ((), (), s32[]{:S(2)}) async-start(), calls=%async_computation.1 | async-start | bytes 9437184 | tf_op jit(solution)/shard_map/all_gather | solution.py:27
  603.1 31.1 %copy-start = (f32[1024,1024]{1,0:T(8,128)S(1)}, f32[1024,1024]{1,0:T(8,128)}, u32[]{:S(2)}) copy-start(f32[1024,1024]{1,0:T(8,128)} %get-tuple-element.57) | copy-start | bytes 12582916 | tf_op jit(solution)/shard_map/conditional.1
  603.1 31.1 %copy-start.3 = (f32[2048,1024]{1,0:T(8,128)S(1)}, f32[2048,1024]{1,0:T(8,128)}, u32[]{:S(2)}) copy-start(f32[2048,1024]{1,0:T(8,128)} %get-tuple-element.56) | copy-start | bytes 25165828 | tf_op jit(solution)/shard_map/conditional.1
  603.1 31.1 %copy-start.5 = (bf16[2048,1024]{1,0:T(8,128)(2,1)S(1)}, bf16[2048,1024]{1,0:T(8,128)(2,1)}, u32[]{:S(2)}) copy-start(bf16[2048,1024]{1,0:T(8,128)(2,1)} %get-tuple-element.53) | copy-start | bytes 12582916 | tf_op jit(solution)/shard_map/conditional.1
Sparse Core Ops, SparseCore 0:
  12.2 110.8 all-gather.2
  128.3 193.9 all-reduce.5
  330.4 161.3 all-reduce.3
  494.0 108.8 all-gather.4
where the time goes:
time: 677 us; the launch traced here: 670 us
  waiting for transfers between devices  547 us (81%)
  matrix products  78.7 us (12%)
  between operations  13.4 us (2%)
  other arithmetic  13.3 us (2%)
  local copies, waits for them, and re-layouts  11.3 us (2%)
    psum x2, waiting for transfers between devices, spread(): return lax.psum(kept, axis)  343 us
    all_gather x2, waiting for transfers between devices, gather_factor(): return lax.all_gather(piece, 'grp', axis=0, tiled=True)  204 us
    dot_general x2, matrix products, product(): jnp.dot(left, right, precision=lax.Precision.HIGHEST, preferred_element_t...  60.3 us
    dot_general x3, matrix products, times_transposed(): lax.dot_general(left, right, (((1,), (1,)), ((), ())), precision=lax.Prec...  18.4 us
  transfers between devices with their start and end apart: 4, of which 4 were waited for; matrix products, arithmetic and copies ran while one was open for 5% of the time, Pallas kernels for 0%

commit v1 on v0

--- a/solution.py
+++ b/solution.py
@@ -24,7 +24,9 @@
 
 
 def gather_factor(piece):
-    return lax.all_gather(piece, "grp", axis=0, tiled=True)
+    return jnp.concatenate(
+        lax.all_to_all(jnp.stack([piece] * lax.axis_size("grp")), "grp", 0, 0), axis=0
+    )
 
 
 def body(metric_panels, diag_inverses, pair_batch):

time: 677 us -> 637 us (0.941)
  waiting for transfers between devices: 547 us -> 498 us
  starting transfers between devices: 0.13 us -> 13.9 us
  local copies, waits for them, and re-layouts: 11.3 us -> 19.8 us
    all_gather x2 -> x0, waiting for transfers between devices: 204 us -> none  [gather_factor(): return lax.all_gather(piece, 'grp', axis=0, tiled=True)]
    all_to_all x0 -> x2, waiting for transfers between devices: none -> 101 us  [gather_factor(): lax.all_to_all(jnp.stack([piece] * lax.axis_size('grp')), 'grp', 0, 0)]
    psum x2, waiting for transfers between devices: 343 us -> 396 us  [spread(): return lax.psum(kept, axis)]
    all_to_all x0 -> x2, starting transfers between devices: none -> 13.9 us  [gather_factor(): lax.all_to_all(jnp.stack([piece] * lax.axis_size('grp')), 'grp', 0, 0)]
    another operation x6, local copies, waits for them, and re-layouts: 0.01 us -> 8.61 us  [the longest x2 8.6 us: gather_factor(): jnp.stack([piece] * lax.axis_size('grp'))]
  transfers between devices with their start and end apart: 4 -> 4, of which waited for: 4 -> 3; matrix products, arithmetic and copies ran while one was open for 5% -> 3% of each run, Pallas kernels for 0% -> 0%
where the time goes in v1:
time: 637 us
  waiting for transfers between devices  498 us (78%)
  matrix products  78.6 us (12%)
  local copies, waits for them, and re-layouts  19.8 us (3%)
  starting transfers between devices  13.9 us (2%)
  between operations  13.5 us (2%)
  other arithmetic  13.2 us (2%)
    psum x2, waiting for transfers between devices, spread(): return lax.psum(kept, axis)  396 us
    all_to_all x2, waiting for transfers between devices, gather_factor(): lax.all_to_all(jnp.stack([piece] * lax.axis_size('grp')), 'grp', 0, 0)  101 us
    dot_general x2, matrix products, product(): jnp.dot(left, right, precision=lax.Precision.HIGHEST, preferred_element_t...  62.3 us
    dot_general x3, matrix products, times_transposed(): lax.dot_general(left, right, (((1,), (1,)), ((), ())), precision=lax.Prec...  16.3 us
    all_to_all x2, starting transfers between devices, gather_factor(): lax.all_to_all(jnp.stack([piece] * lax.axis_size('grp')), 'grp', 0, 0)  13.9 us
  transfers between devices with their start and end apart: 4, of which 3 were waited for; matrix products, arithmetic and copies ran while one was open for 3% of the time, Pallas kernels for 0%

profile of v1, /device:TPU:1, one launch (start us, length us, event | category | flops | bytes accessed | tf_op | source)
XLA Modules:
  0.0 636.9 jit_solution(11102831689402082281)
XLA Ops:
  6.5 4.5 fusion.8
  11.1 4.3 stack.4
  15.4 8.2 %all-to-all-start = ((f32[8,256,1024]{2,1,0:T(8,128)}), f32[8,256,1024]{2,1,0:T(8,128)}, u32[]{:S(2)}, u32[]{:S(2)}) async-start(f32[8,256,1024]{2,1,0:T(8,128)} %stack.4), calls=%async_computation | async-start | bytes 16777216 | tf_op jit(solution)/shard_map/all_to_all | solution.py:28
  23.5 0.0 all-reduce.6.cloned.1.call-start
  23.6 8.5 %slice_bitcast_fusion = (f32[1024,1024]{1,0:T(8,128)}, f32[1024,1024]{1,0:T(8,128)}) fusion(f32[2,1024,1024]{2,1,0:T(8,128)} %param.10), kind=kLoop, calls=%fused_computation.10 | loop fusion | bytes 16777216 | tf_op jit(solution)/shard_map/squeeze | solution.py:37
  32.0 2.5 conditional.8
  32.0 2.5 broadcast_in_dim.12
  34.6 2.8 broadcast_select_fusion
  37.3 101.4 %all-to-all-done = f32[8,256,1024]{2,1,0:T(8,128)} async-done(((f32[8,256,1024]{2,1,0:T(8,128)}), f32[8,256,1024]{2,1,0:T(8,128)}, u32[]{:S(2)}, u32[]{:S(2)}) %all-to-all-start) | async-done | bytes 8388640 | tf_op jit(solution)/shard_map/all_to_all | solution.py:28
  138.7 5.0 slice_select_fusion
  143.7 0.0 all-reduce.6.cloned.1.call-update
  143.7 196.5 %all-reduce.6.cloned.1.call-done = (f32[1024,1024]{1,0:T(8,128)}, f32[1024,1024]{1,0:T(8,128)}) async-done(((f32[1024,1024]{1,0:T(8,128)}, f32[1024,1024]{1,0:T(8,128)}), (f32[1024,1024]{1,0:T(8,128)}, f32[1024,1024]{1,0:T(8,128)})) %all-reduce.6.cloned.1.call-update) | async-done | bytes 8388624 | tf_op jit(solution)/shard_map/psum | solution.py:9
  340.2 6.0 convolution_subtract_fusion
  346.2 5.7 fusion.11
  352.0 4.3 stack.5
  356.3 5.7 all-to-all-start.1
  362.0 0.0 all-reduce.4.cloned.1.call-start
  362.0 0.5 conditional.9
  362.0 0.3 broadcast_in_dim.13.clone
  362.6 1.5 broadcast_select_fusion.1
  364.0 0.0 all-reduce.4.cloned.1.call-update
  364.0 199.7 %all-reduce.4.cloned.1.call-done = bf16[1024,1024]{1,0:T(8,128)(2,1)} async-done(((bf16[1024,1024]{1,0:T(8,128)(2,1)}), bf16[1024,1024]{1,0:T(8,128)(2,1)}) %all-reduce.4.cloned.1.call-update) | async-done | bytes 2097168 | tf_op jit(solution)/shard_map/psum | solution.py:9
  563.8 4.0 convert_element_type.40
  567.8 0.0 all-to-all-done.1
  567.8 62.3 %conditional.10 = (bf16[2048,1024]{1,0:T(8,128)(2,1)}) conditional(s32[]{:T(128)} %convert_element_type.39, (bf16[2048,1024]{1,0:T(8,128)(2,1)}, f32[8,256,1024]{2,1,0:T(8,128)}, f32[1024,1024]{1,0:T(8,128)}, f32[8,256,1024]{2,1,0:T(8,128)}, f32[1024,1024]{1,0:T(8,128)}) %tuple.39, (f32[1024,1024]{1,0:T(8,128)}, f32[1024,1024]{1,0:T(8,128)}) %tuple.40), branch_computations={%region_7.8_spmd, %region_8.9_spmd} | conditional | flops 51547996160 | bytes 83886144
  567.8 0.0 copy-start
  567.8 0.0 copy-start.3
  567.8 31.1 %fusion.13 = f32[2048,1024]{1,0:T(8,128)S(1)} fusion(f32[2048,1024]{1,0:T(8,128)} %bitcast.1, f32[1024,1024]{1,0:T(8,128)} %get-tuple-element.55), kind=kOutput, calls=%fused_computation.20 | convolution fusion | flops 25769803776 | bytes 20971520 | tf_op jit(solution)/shard_map/cond/branch_0_fun/dot_general | solution.py:23
  598.8 0.0 copy-done
  598.8 0.0 copy-done.3
  598.8 31.3 %subtract_subtract_fusion = bf16[2048,1024]{1,0:T(8,128)(2,1)} fusion(f32[2048,1024]{1,0:T(8,128)S(1)} %fusion.13, bf16[2048,1024]{1,0:T(8,128)(2,1)S(1)} %copy-done.3, f32[2048,1024]{1,0:T(8,128)} %bitcast.2, f32[1024,1024]{1,0:T(8,128)S(1)} %copy-done), kind=kOutput, calls=%fused_computation.7 | convolution fusion | flops 25778192384 | bytes 29360128 | tf_op jit(solution)/shard_map/cond/branch_0_fun/dot_general | solution.py:23
Async XLA Ops:
  15.4 123.3 %all-to-all-start = ((f32[8,256,1024]{2,1,0:T(8,128)}), f32[8,256,1024]{2,1,0:T(8,128)}, u32[]{:S(2)}, u32[]{:S(2)}) async-start(f32[8,256,1024]{2,1,0:T(8,128)} %stack.4), calls=%async_computation | async-start | bytes 16777216 | tf_op jit(solution)/shard_map/all_to_all | solution.py:28
  23.5 316.7 %all-reduce.6.cloned.1.call-start = ((), (), s32[]{:S(2)}) async-start(), calls=%async_computation.3 | async-start | bytes 16777216 | tf_op jit(solution)/shard_map/psum | solution.py:9
  356.3 211.5 %all-to-all-start.1 = ((f32[8,256,1024]{2,1,0:T(8,128)}), f32[8,256,1024]{2,1,0:T(8,128)}, u32[]{:S(2)}, u32[]{:S(2)}) async-start(f32[8,256,1024]{2,1,0:T(8,128)} %stack.5), calls=%async_computation.1 | async-start | bytes 16777216 | tf_op jit(solution)/shard_map/all_to_all | solution.py:28
  362.0 201.8 %all-reduce.4.cloned.1.call-start = ((), (), s32[]{:S(2)}) async-start(), calls=%async_computation.2 | async-start | bytes 4194304 | tf_op jit(solution)/shard_map/psum | solution.py:9
  567.8 31.1 %copy-start = (f32[1024,1024]{1,0:T(8,128)S(1)}, f32[1024,1024]{1,0:T(8,128)}, u32[]{:S(2)}) copy-start(f32[1024,1024]{1,0:T(8,128)} %get-tuple-element.57) | copy-start | bytes 12582916 | tf_op jit(solution)/shard_map/conditional.1
  567.8 31.1 %copy-start.3 = (bf16[2048,1024]{1,0:T(8,128)(2,1)S(1)}, bf16[2048,1024]{1,0:T(8,128)(2,1)}, u32[]{:S(2)}) copy-start(bf16[2048,1024]{1,0:T(8,128)(2,1)} %get-tuple-element.53) | copy-start | bytes 12582916 | tf_op jit(solution)/shard_map/conditional.1
Sparse Core Ops, SparseCore 0:
  143.8 196.2 all-reduce.5
  365.3 198.4 all-reduce.3
